TPU v7x, 512 devices: a whole 4x4x16 slice. The times are simulated.
512 devices in a mesh: wide: 32 (over z_lo, x), narrow: 16 (over z_hi, y, core).
Axes of the slice: x: 4, y: 4, z: 16 (z_hi: 2, z_lo: 8; z = z_hi * 8 + z_lo), core: 2. Of those that a mesh axis runs over, the one named last changes fastest.
Arguments:
- jacobian: bfloat16 [2048, 16384], P(None, ('wide', 'narrow')), may hold values from -0.125 to 0.125
- variance: float32 [2048], replicated, may hold values from 0.1 to 10
Outputs:
- hessian: float32 [16384, 16384], P('wide', 'narrow')
All inputs are finite; a program needn't handle non-finite values.
Results may differ from a plain program's by a relative error of at most 0.004.
Values may be sent and summed in bfloat16 or wider, within the bound.
A program may use at most 64 MiB of HBM per device.

v0:
```python
import jax
import jax.numpy as jnp
from jax import lax
from jax.sharding import PartitionSpec as P

BLOCKS = 2


def laid_out(tiles, dim):
    tiles = jnp.moveaxis(tiles, 0, dim)
    shape = tiles.shape
    return tiles.reshape(*shape[:dim], shape[dim] * shape[dim + 1], *shape[dim + 2 :])


def copy_for_each(x, axis):
    copies = jnp.broadcast_to(x, (lax.axis_size(axis), *x.shape))
    return lax.all_to_all(copies, axis, split_axis=0, concat_axis=0, tiled=True)


def gathered_copies(x, axis, dim):
    return laid_out(copy_for_each(x, axis), dim)


def weigh(panel, row_scale):
    return (panel.astype(jnp.float32) * row_scale).astype(jnp.bfloat16)


def contract(left_panel, right_panel):
    return lax.dot_general(
        left_panel, right_panel, (((0,), (0,)), ((), ())), preferred_element_type=jnp.float32
    )


def body(jacobian, variance):
    panel_ratio = lax.axis_size("wide") // lax.axis_size("narrow")
    first_root = lax.axis_index("narrow") * panel_ratio
    block_rows = jacobian.shape[0] // BLOCKS
    weights = lax.rsqrt(variance)
    hessian_tile = None
    for block in range(BLOCKS):
        block_jac = jacobian[block * block_rows : (block + 1) * block_rows]
        row_scale = weights[block * block_rows : (block + 1) * block_rows][:, None]
        scaled_local = weigh(block_jac, row_scale)
        rows_panel = lax.all_gather(scaled_local, "narrow", axis=1, tiled=True)
        panel_width = rows_panel.shape[1]
        pieces = lax.all_to_all(rows_panel, "wide", split_axis=0, concat_axis=1, tiled=True)
        chosen = lax.dynamic_slice_in_dim(
            pieces, first_root * panel_width, panel_ratio * panel_width, 1
        )
        columns = gathered_copies(chosen, "wide", 0)
        products = contract(rows_panel, columns)
        hessian_tile = products if hessian_tile is None else hessian_tile + products
    return hessian_tile


def solution(mesh):
    placed = (P(None, ("wide", "narrow")), P())
    return jax.shard_map(
        body, mesh=mesh, in_specs=placed, out_specs=P("wide", "narrow"), check_vma=False
    )
```

profile of v0, /device:TPU:25, one launch (start us, length us, event | category | flops | bytes accessed | tf_op | source)
XLA Modules:
  0.0 465.5 jit_solution(16100780816616694054)
XLA Ops:
  6.5 0.0 all-gather.3.cloned.1.call-start
  6.5 0.7 rsqrt.3
  7.2 1.6 multiply_convert_fusion
  8.8 0.0 all-gather.3.cloned.1.call-update
  8.8 83.9 %all-gather.3.cloned.1.call-done = bf16[1024,512]{0,1:T(8,128)(2,1)} async-done(((bf16[1024,32]{0,1:T(8,128)(2,1)}), bf16[1024,512]{0,1:T(8,128)(2,1)}) %all-gather.3.cloned.1.call-update) | async-done | bytes 1048592 | tf_op jit(solution)/shard_map/all_gather | solution.py:44
  92.7 2.3 copy.7
  95.0 4.8 %all-to-all-start = ((bf16[32,32,512]{2,1,0:T(8,128)(2,1)}), bf16[32,32,512]{2,1,0:T(8,128)(2,1)S(1)}, u32[]{:S(2)}, u32[]{:S(2)}) async-start(bf16[32,32,512]{2,1,0:T(8,128)(2,1)} %bitcast), calls=%async_computation | async-start | bytes 2097152 | tf_op jit(solution)/shard_map/all_to_all | solution.py:46
  99.7 0.0 all-gather.5.cloned.1.call-start
  99.8 0.7 all-gather.5.cloned.1.call-update
  100.5 88.1 %all-gather.5.cloned.1.call-done = bf16[1024,512]{0,1:T(8,128)(2,1)} async-done(((bf16[1024,32]{0,1:T(8,128)(2,1)}), bf16[1024,512]{0,1:T(8,128)(2,1)}) %all-gather.5.cloned.1.call-update) | async-done | bytes 1048592 | tf_op jit(solution)/shard_map/all_gather | solution.py:44
  188.6 2.3 copy.9
  190.9 0.0 all-to-all-done
  190.9 4.8 %all-to-all-start.2 = ((bf16[32,32,512]{2,1,0:T(8,128)(2,1)}), bf16[32,32,512]{2,1,0:T(8,128)(2,1)S(1)}, u32[]{:S(2)}, u32[]{:S(2)}) async-start(bf16[32,32,512]{2,1,0:T(8,128)(2,1)} %bitcast.3), calls=%async_computation.2 | async-start | bytes 2097152 | tf_op jit(solution)/shard_map/all_to_all | solution.py:46
  195.7 0.1 copy.11
  195.8 50.0 %all-to-all-done.2 = bf16[32,32,512]{2,1,0:T(8,128)(2,1)S(1)} async-done(((bf16[32,32,512]{2,1,0:T(8,128)(2,1)}), bf16[32,32,512]{2,1,0:T(8,128)(2,1)S(1)}, u32[]{:S(2)}, u32[]{:S(2)}) %all-to-all-start.2) | async-done | bytes 1048608 | tf_op jit(solution)/shard_map/all_to_all | solution.py:46
  245.8 1.6 broadcast_in_dim.8
  247.4 7.9 %all-to-all-start.1 = ((bf16[32,32,1024]{2,1,0:T(8,128)(2,1)}), bf16[32,32,1024]{2,1,0:T(8,128)(2,1)}, u32[]{:S(2)}, u32[]{:S(2)}) async-start(bf16[32,32,1024]{2,1,0:T(8,128)(2,1)} %broadcast_in_dim.8), calls=%async_computation.1 | async-start | bytes 4194304 | tf_op jit(solution)/shard_map/all_to_all | solution.py:17
  255.3 0.1 copy.12
  255.4 94.5 %all-to-all-done.1 = bf16[32,32,1024]{2,1,0:T(8,128)(2,1)} async-done(((bf16[32,32,1024]{2,1,0:T(8,128)(2,1)}), bf16[32,32,1024]{2,1,0:T(8,128)(2,1)}, u32[]{:S(2)}, u32[]{:S(2)}) %all-to-all-start.1) | async-done | bytes 2097184 | tf_op jit(solution)/shard_map/all_to_all | solution.py:17
  349.9 1.6 broadcast_in_dim.9
  351.5 0.0 copy-start
  351.5 8.0 %all-to-all-start.3 = ((bf16[32,32,1024]{2,1,0:T(8,128)(2,1)}), bf16[32,32,1024]{2,1,0:T(8,128)(2,1)S(1)}, u32[]{:S(2)}, u32[]{:S(2)}) async-start(bf16[32,32,1024]{2,1,0:T(8,128)(2,1)} %broadcast_in_dim.9), calls=%async_computation.3 | async-start | bytes 4194304 | tf_op jit(solution)/shard_map/all_to_all | solution.py:17
  359.5 0.0 copy-done
  359.5 4.2 fusion.1
  363.7 90.5 %all-to-all-done.3 = bf16[32,32,1024]{2,1,0:T(8,128)(2,1)S(1)} async-done(((bf16[32,32,1024]{2,1,0:T(8,128)(2,1)}), bf16[32,32,1024]{2,1,0:T(8,128)(2,1)S(1)}, u32[]{:S(2)}, u32[]{:S(2)}) %all-to-all-start.3) | async-done | bytes 2097184 | tf_op jit(solution)/shard_map/all_to_all | solution.py:17
  454.1 4.5 convolution_add_fusion
  (3 shorter events, 0.0 us)
Async XLA Ops:
  6.5 86.2 %all-gather.3.cloned.1.call-start = ((), (), s32[]{:S(2)}) async-start(), calls=%async_computation.4 | async-start | bytes 1114112 | tf_op jit(solution)/shard_map/all_gather | solution.py:44
  95.0 96.0 %all-to-all-start = ((bf16[32,32,512]{2,1,0:T(8,128)(2,1)}), bf16[32,32,512]{2,1,0:T(8,128)(2,1)S(1)}, u32[]{:S(2)}, u32[]{:S(2)}) async-start(bf16[32,32,512]{2,1,0:T(8,128)(2,1)} %bitcast), calls=%async_computation | async-start | bytes 2097152 | tf_op jit(solution)/shard_map/all_to_all | solution.py:46
  99.7 88.9 %all-gather.5.cloned.1.call-start = ((), (), s32[]{:S(2)}) async-start(), calls=%async_computation.5 | async-start | bytes 1114112 | tf_op jit(solution)/shard_map/all_gather | solution.py:44
  190.9 54.9 %all-to-all-start.2 = ((bf16[32,32,512]{2,1,0:T(8,128)(2,1)}), bf16[32,32,512]{2,1,0:T(8,128)(2,1)S(1)}, u32[]{:S(2)}, u32[]{:S(2)}) async-start(bf16[32,32,512]{2,1,0:T(8,128)(2,1)} %bitcast.3), calls=%async_computation.2 | async-start | bytes 2097152 | tf_op jit(solution)/shard_map/all_to_all | solution.py:46
  247.4 102.5 %all-to-all-start.1 = ((bf16[32,32,1024]{2,1,0:T(8,128)(2,1)}), bf16[32,32,1024]{2,1,0:T(8,128)(2,1)}, u32[]{:S(2)}, u32[]{:S(2)}) async-start(bf16[32,32,1024]{2,1,0:T(8,128)(2,1)} %broadcast_in_dim.8), calls=%async_computation.1 | async-start | bytes 4194304 | tf_op jit(solution)/shard_map/all_to_all | solution.py:17
  351.5 8.0 %copy-start = (bf16[1024,512]{0,1:T(8,128)(2,1)S(1)}, bf16[1024,512]{0,1:T(8,128)(2,1)}, u32[]{:S(2)}) copy-start(bf16[1024,512]{0,1:T(8,128)(2,1)} %all-gather.3.cloned.1.call-done) | copy-start | bytes 3145732
  351.5 102.7 %all-to-all-start.3 = ((bf16[32,32,1024]{2,1,0:T(8,128)(2,1)}), bf16[32,32,1024]{2,1,0:T(8,128)(2,1)S(1)}, u32[]{:S(2)}, u32[]{:S(2)}) async-start(bf16[32,32,1024]{2,1,0:T(8,128)(2,1)} %broadcast_in_dim.9), calls=%async_computation.3 | async-start | bytes 4194304 | tf_op jit(solution)/shard_map/all_to_all | solution.py:17
Sparse Core Ops, SparseCore 0:
  10.6 81.9 all-gather.2
  103.9 84.7 all-gather.4
where the time goes:
time: 468 us; the launch traced here: 465 us
  waiting for transfers between devices  408 us (87%)
  starting transfers between devices  25.5 us (5%)
  between operations  13.5 us (3%)
  matrix products  8.66 us (2%)
  local copies, waits for them, and re-layouts  8.64 us (2%)
    all_to_all x2, waiting for transfers between devices, copy_for_each(): return lax.all_to_all(copies, axis, split_axis=0, concat_axis=0, tiled=True)  185 us
    all_gather x2, waiting for transfers between devices, body(): rows_panel = lax.all_gather(scaled_local, 'narrow', axis=1, tiled=True)  172 us
    all_to_all x2, waiting for transfers between devices, body(): lax.all_to_all(rows_panel, 'wide', split_axis=0, concat_axis=1, tiled=True)  50 us
    all_to_all x2, starting transfers between devices, copy_for_each(): return lax.all_to_all(copies, axis, split_axis=0, concat_axis=0, tiled=True)  15.9 us
    all_to_all x2, starting transfers between devices, body(): lax.all_to_all(rows_panel, 'wide', split_axis=0, concat_axis=1, tiled=True)  9.53 us
  transfers between devices with their start and end apart: 6, of which 5 were waited for; matrix products, arithmetic and copies ran while one was open for 1% of the time, Pallas kernels for 0%

commit v1 on v0

v1 whole, which is shorter than its diff:
```python
import jax
import jax.numpy as jnp
from jax import lax
from jax.experimental import pallas as pl
from jax.experimental.pallas import tpu as pltpu
from jax.sharding import PartitionSpec as P

MESH = pl.DeviceIdType.MESH
XS, ZS, YS, HALVES, CORES = 4, 8, 4, 2, 2
PIECES = 8
LAST = ZS - 1
KAPPA = 2
FAR_LAG = 3
SIB_LAG = 2
GATHER_AT = (10, 12, 14)
STEPS = 8 + 8 + SIB_LAG + 1


def kernel(
    jac_ref, var_ref, out_ref, row, col, acc,
    row_recv, col_recv, send_y, send_e, send_f, send_z, send_x, out_sem,
):
    width = jac_ref.shape[0]
    half = width // 2
    panel = 2 * PIECES * width
    wide, narrow = lax.axis_index("wide"), lax.axis_index("narrow")
    x, zl = lax.rem(wide, XS), lax.div(wide, XS)
    core = lax.rem(narrow, CORES)
    y = lax.rem(lax.div(narrow, CORES), YS)
    zh = lax.div(narrow, CORES * YS)
    odd = lax.rem(x, 2)
    own_plane = zh * YS + y
    primary = lax.div(x, 2) == core
    primary_i = primary.astype(jnp.int32)

    def device(x=x, y=y, zh=zh, zl=zl, core=core):
        return (zl * XS + x, (zh * YS + y) * CORES + core)

    up_y, down_y = lax.rem(y + 1, YS), lax.rem(y + YS - 1, YS)
    far_y = lax.rem(y + 2, YS)
    sibling = device(core=1 - core)
    above, below = device(y=up_y), device(y=down_y)
    opposite = device(zh=1 - zh)
    partner = device(x=x + 1 - 2 * odd)
    other = device(x=lax.rem(x + XS - 1 + 2 * odd, XS))
    near_source = primary & (zl == own_plane)
    far_source = primary & (zl == (1 - zh) * YS + y)
    line_end = primary & (zl == LAST * (1 - zh))
    entry = device(zh=1 - zh, zl=LAST * zh)
    entry_from = device(zh=1 - zh, zl=zh * YS + y)
    z_up, z_down = device(zl=zl + 1), device(zl=zl - 1)
    can_up, can_down = primary & (zl < LAST), primary & (zl > 0)
    k_own = jnp.where(primary, odd, 1 - odd)
    k_other = 1 - k_own

    def piece(h, py, pc):
        return (h * YS + py) * CORES + pc

    def row_at(i, start=0, size=None):
        return row.at[pl.ds(pl.multiple_of(i * width + start, half), size or width)]

    def col_at(k, i):
        return col.at[pl.ds(pl.multiple_of(k * panel + i * width, width), width)]

    def remote(src, dst, send, recv, to):
        return pltpu.make_async_remote_copy(
            src_ref=src, dst_ref=dst, send_sem=send, recv_sem=recv, device_id=to, device_id_type=MESH
        )

    def row_copy(i, send, to, part=0, start=0, size=None):
        ref = row_at(i, start, size)
        return remote(ref, ref, send, row_recv.at[i, part], to)

    def col_copy(k, i, send, to):
        ref = col_at(k, i)
        return remote(ref, ref, send, col_recv.at[k, i], to)

    scale = lax.rsqrt(var_ref[...])
    mine = piece(zh, y, core)
    row_at(mine)[...] = (jac_ref[...].astype(jnp.float32) * scale).astype(jnp.bfloat16)

    barrier = pltpu.get_barrier_semaphore()
    for to in (sibling, above, below, opposite, partner, other):
        pl.semaphore_signal(barrier, inc=1, device_id=to, device_id_type=MESH)
    for present, to in ((can_up, z_up), (can_down, z_down), (far_source, entry), (line_end, entry_from)):

        @pl.when(present)
        def _():
            pl.semaphore_signal(barrier, inc=1, device_id=to, device_id_type=MESH)

    expected = 6 + sum(p.astype(jnp.int32) for p in (can_up, can_down, far_source, line_end))
    pl.semaphore_wait(barrier, expected)

    def y_copies(hi, h):
        own, lo, up, far = (piece(h, v, core) for v in (y, down_y, up_y, far_y))
        sems = [send_y.at[hi, i] for i in range(8)]
        return dict(
            own_up=row_copy(own, sems[0], above),
            own_down=row_copy(own, sems[1], below),
            own_sib=row_copy(own, sems[2], sibling),
            lo_up=row_copy(lo, sems[3], above, 0, 0, half),
            lo_sib=row_copy(lo, sems[4], sibling),
            up_down=row_copy(up, sems[5], below, 1, half, half),
            up_sib=row_copy(up, sems[6], sibling),
            far_sib=row_copy(far, sems[7], sibling),
            far_lo=row_copy(far, sems[7], above, 0, 0, half),
            far_hi=row_copy(far, sems[7], below, 1, half, half),
        )

    near_y, far_rows = y_copies(0, zh), y_copies(1, 1 - zh)

    def gather_own(cp):
        cp["own_up"].start()
        cp["own_down"].start()
        cp["own_sib"].start()

    def gather_up(cp):
        cp["up_sib"].wait_recv()
        cp["up_down"].start()
        cp["up_sib"].start()

    def gather_low(cp):
        cp["lo_sib"].wait_recv()
        cp["lo_up"].start()
        cp["lo_sib"].start()

    def gather_far(cp):
        cp["far_lo"].wait_recv()
        cp["far_hi"].wait_recv()
        cp["far_sib"].start()

    exchange = row_copy(mine, send_e.at[0], opposite)
    exchanged = piece(1 - zh, y, core)

    def order(h, j):
        q = lax.div(j, 2)
        turn = q + lax.div(q, 2) - 2 * lax.div(q, 3)
        return piece(h, lax.rem(y + turn, YS), lax.rem(core + j, CORES))

    def sib_wait(h, py):
        row_copy(piece(h, py, 1 - core), send_y.at[0, 0], sibling).wait_recv()

    def feed(j):
        i = order(zh, jnp.int32(j))

        @pl.when(near_source)
        def _():
            pltpu.make_async_copy(row_at(i), col_at(odd, i), col_recv.at[odd, i]).start()

        @pl.when(far_source)
        def _():
            remote(row_at(i), col_at(odd, i), send_f.at[j], col_recv.at[odd, i], entry).start()

    source = near_source | far_source

    def feed_sib(j, py):
        @pl.when(source)
        def _():
            sib_wait(zh, py)

        feed(j)

    gather_own(near_y)
    exchange.start()
    feed(0)
    feed_sib(1, y)
    gather_up(near_y)
    feed(2)
    gather_low(near_y)
    feed_sib(3, up_y)
    feed(4)
    feed_sib(5, down_y)
    gather_far(near_y)
    feed(6)
    feed_sib(7, far_y)

    hops_near = jnp.maximum(zl - own_plane, own_plane - zl)
    hops_far = jnp.where(zh == 0, LAST - zl, zl)
    at_near, at_far = KAPPA * hops_near, KAPPA * hops_far + FAR_LAG
    first = jnp.minimum(at_near, at_far)
    lag_near = jnp.minimum(at_near - first, PIECES)
    lag_far = jnp.minimum(at_far - first, PIECES)

    z_near_up, z_near_down = can_up & (zl >= own_plane), can_down & (zl <= own_plane)
    z_far_up, z_far_down = can_up & (zh == 1), can_down & (zh == 0)
    types = ((0, zh, lag_near, z_near_up, z_near_down), (1, 1 - zh, lag_far, z_far_up, z_far_down))

    def sends(t, h, j, up, down):
        i = order(h, j)
        slot = t * PIECES + j
        relay_own = primary | (lax.rem(j, 2) == 1)
        return (
            (up, col_copy(k_own, i, send_z.at[0, slot], z_up)),
            (down, col_copy(k_own, i, send_z.at[1, slot], z_down)),
            (primary, col_copy(k_own, i, send_x.at[0, slot], other)),
            (relay_own, col_copy(k_own, i, send_x.at[1, slot], partner)),
        )

    def relays(t, h, j):
        i = order(h, j)
        return primary & (lax.rem(j, 2) == 0), col_copy(k_other, i, send_x.at[2, t * PIECES + j], other)

    def step(s, carry):
        for t, h, lag, up, down in types:
            j = s - lag

            @pl.when((j >= 0) & (j < PIECES))
            def _():
                col_copy(k_own, order(h, j), send_f.at[0], other).wait_recv()
                for present, cp in sends(t, h, j, up, down):
                    pl.when(present)(cp.start)

        for t, h, lag, up, down in types:
            j = s - lag - SIB_LAG

            @pl.when(primary & (j >= 0) & (j < PIECES))
            def _():
                present, cp = relays(t, h, j)
                cp.wait_recv()
                pl.when(present)(cp.start)

        @pl.when(s == GATHER_AT[0] - first)
        def _():
            row_copy(exchanged, send_e.at[0], opposite).wait_recv()
            gather_own(far_rows)

        @pl.when(s == GATHER_AT[1] - first)
        def _():
            gather_up(far_rows)
            gather_low(far_rows)

        @pl.when(s == GATHER_AT[2] - first)
        def _():
            gather_far(far_rows)

        return carry

    lax.fori_loop(0, STEPS, step, 0)

    @pl.when(jnp.logical_not(source))
    def _():
        for py in (y, up_y, down_y, far_y):
            sib_wait(zh, py)

    for py in (y, up_y, down_y, far_y):
        sib_wait(1 - zh, py)

    def late(s, carry):
        @pl.when(jnp.logical_not(primary))
        def _():
            col_copy(k_other, s, send_f.at[0], other).wait_recv()

        return carry

    lax.fori_loop(0, 2 * PIECES, late, 0)

    block = PIECES * width

    def out_copy(b):
        at = pl.ds(pl.multiple_of(b * block, block), block)
        return pltpu.make_async_copy(acc.at[:, at], out_ref.at[:, at], out_sem.at[b])

    def multiply(b, carry):
        at = pl.ds(pl.multiple_of(b * block, block), block)
        acc[:, at] = lax.dot_general(
            row[...], col[at, :], (((1,), (1,)), ((), ())), preferred_element_type=jnp.float32
        )
        out_copy(b).start()
        return carry

    lax.fori_loop(0, 4, multiply, 0)

    for cp in (near_y, far_rows):
        for name in ("own_up", "own_down", "own_sib", "lo_up", "lo_sib", "up_down", "up_sib", "far_sib"):
            cp[name].wait_send()
    exchange.wait_send()

    @pl.when(far_source)
    def _():
        for j in range(PIECES):
            i = order(zh, jnp.int32(j))
            remote(row_at(i), col_at(odd, i), send_f.at[j], col_recv.at[odd, i], entry).wait_send()

    def drain(j, carry):
        for t, h, lag, up, down in types:
            for present, cp in (*sends(t, h, j, up, down), relays(t, h, j)):
                pl.when(present)(cp.wait_send)
        return carry

    lax.fori_loop(0, PIECES, drain, 0)
    for b in range(4):
        out_copy(b).wait()


def body(jacobian, variance):
    depth, width = jacobian.shape
    rows, columns = 2 * PIECES * width, 4 * PIECES * width
    vmem = pl.BlockSpec(memory_space=pltpu.VMEM)
    dma = pltpu.SemaphoreType.DMA
    return pl.pallas_call(
        kernel,
        out_shape=jax.ShapeDtypeStruct((rows, columns), jnp.float32),
        in_specs=[vmem, vmem],
        out_specs=pl.BlockSpec(memory_space=pl.ANY),
        scratch_shapes=[
            pltpu.VMEM((rows, depth), jnp.bfloat16),
            pltpu.VMEM((columns, depth), jnp.bfloat16),
            pltpu.VMEM((rows, columns), jnp.float32),
            dma((16, 2)), dma((2, 16)), dma((2, 8)), dma((1,)), dma((8,)), dma((2, 16)), dma((3, 16)), dma((4,)),
        ],
        compiler_params=pltpu.CompilerParams(collective_id=0, has_side_effects=True),
    )(jacobian.T, variance.reshape(1, depth))


def solution(mesh):
    placed = (P(None, ("wide", "narrow")), P())
    return jax.shard_map(
        body, mesh=mesh, in_specs=placed, out_specs=P("wide", "narrow"), check_vma=False
    )
```

time: 468 us -> 107 us (0.23)
  the two profiles are of different devices: /device:TPU:25 before, /device:TPU:28 now
where the time goes in v1:
time: 107 us
  Pallas kernels  104 us (97%)
  local copies, waits for them, and re-layouts  3.16 us (3%)
    pallas_call x1, Pallas kernels, body(): pl.pallas_call(kernel, out_shape=jax.ShapeDtypeStruct((rows, columns), jn...  104 us
    unnamed x1, local copies, waits for them, and re-layouts  3.16 us

profile of v1, /device:TPU:28, one launch (start us, length us, event | category | flops | bytes accessed | tf_op | source)
XLA Modules:
  0.0 106.9 jit_solution(16985191210903572094)
XLA Ops:
  0.0 103.7 %shard_map.28 = f32[512,1024]{1,0:T(8,128)} custom-call(bf16[32,2048]{1,0:T(8,128)(2,1)} %bitcast.2, f32[1,2048]{1,0:T(1,128)} %bitcast.3), custom_call_target="tpu_custom_call" | custom-call | tf_op jit(solution)/shard_map/pallas_call | solution.py:300
  103.7 3.2 %copy.4 = f32[512,1024]{1,0:T(8,128)} copy(f32[512,1024]{1,0:T(8,128)} %shard_map.28) | data formatting | bytes 4194304
